TPU v7x, 128 devices: a whole 4x4x4 slice. The times are simulated.
128 devices in a mesh: row: 8 (over x, core), col: 16 (over z, y).
Axes of the slice: x: 4, y: 4, z: 4, core: 2. Of those that a mesh axis runs over, the one named last changes fastest.
Arguments:
- embeddings: bfloat16 [32768, 1024], P(('row', 'col')), may hold values from -6 to 6
- features: bfloat16 [32768, 256], P(('row', 'col')), may hold values from -6 to 6
- candidates: int32 [256, 38], P(('row', 'col')), may hold values from 0 to 255, as said below
Outputs:
- smoothed: bfloat16 [32768, 256], P(('row', 'col'))
Inputs may be any that keep to these rules, and one draw needn't show every extreme that they name: `candidates`: each row names 38 distinct blocks. Over the blocks held by one row of devices, the entries that name blocks held by one column of devices number at most 160, and in every row of devices some column reaches that number.
All inputs are finite; a program needn't handle non-finite values.
Results may differ from a plain program's by a relative error of at most 0.012.
The roundings to bfloat16 on the way count: a program that leaves them out, or rounds other values in their place, can miss the bound.
Values may be sent and summed in bfloat16 or wider, within the bound.
No kernel may reach another device: no remote copies, remote signals or barrier semaphores. Data moves between devices by JAX's collectives and lax.ppermute only.
A program may use at most 128 MiB of HBM per device.

v0:
```python
import jax
import jax.numpy as jnp
from jax import lax
from jax.sharding import PartitionSpec as P

EMB = 1024
FEAT = 256
BLOCK = 128
NB_DEV = 2
BETA = 16


def unit_rows(embeddings):
    values = embeddings.astype(jnp.float32)
    factor = lax.rsqrt(jnp.mean(values * values, axis=1, keepdims=True) + 1e-06) * values.shape[
        1
    ] ** (-0.5)
    return (values * factor).astype(jnp.bfloat16)


def pair_lists(keep, cand_local, query_ids, block_lists):
    query_blocks, list_len = keep.shape
    kept_int = keep.astype(jnp.int32)
    rank = jnp.cumsum(kept_int, axis=1) - 1
    destination = jnp.where(keep, rank, list_len)
    query_rows = jnp.broadcast_to(
        jnp.arange(query_blocks, dtype=jnp.int32)[:, None], (query_blocks, list_len)
    )
    same_flag = (block_lists == query_ids[:, None]).astype(jnp.int32)
    blank_table = jnp.zeros((query_blocks, list_len), jnp.int32)
    cand_sel = blank_table.at[query_rows, destination].set(cand_local, mode="drop")
    same_sel = blank_table.at[query_rows, destination].set(same_flag, mode="drop")
    counts = jnp.sum(kept_int, axis=1)
    return (cand_sel, same_sel, counts)


def smooth_tile(query_units, cand_units, cand_feats, cand_sel, same_sel, counts):
    query_blocks, block_len, _ = query_units.shape
    feat_width = cand_feats.shape[2]
    diagonal_mask = jnp.eye(block_len, dtype=jnp.bool_)

    def turn(slot, state):
        numerator, denominator = state
        cand_idx = lax.dynamic_slice_in_dim(cand_sel, slot, 1, 1)[:, 0]
        same_idx = lax.dynamic_slice_in_dim(same_sel, slot, 1, 1)[:, 0]
        active = (slot < counts).astype(jnp.float32)
        cand_blk = jnp.take(cand_units, cand_idx, axis=0)
        feat_blk = jnp.take(cand_feats, cand_idx, axis=0)
        cosine = jnp.einsum(
            "qie,qje->qij", query_units, cand_blk, preferred_element_type=jnp.float32
        )
        weight = jnp.exp(BETA * (cosine - 1.0))
        is_self = jnp.logical_and(same_idx[:, None, None] > 0, diagonal_mask[None])
        weight = jnp.where(is_self, jnp.float32(0.0), weight) * active[:, None, None]
        numerator = numerator + jnp.einsum(
            "qij,qjf->qif",
            weight.astype(jnp.bfloat16),
            feat_blk,
            preferred_element_type=jnp.float32,
        )
        denominator = denominator + jnp.sum(weight, axis=2)
        return (numerator, denominator)

    turn_count = jnp.max(counts)
    initial = (
        jnp.zeros((query_blocks, block_len, feat_width), jnp.float32),
        jnp.zeros((query_blocks, block_len), jnp.float32),
    )
    return lax.fori_loop(0, turn_count, turn, initial)


def on_device(embeddings, features, candidates):
    units = unit_rows(embeddings)
    row_index = lax.axis_index("row")
    col_index = lax.axis_index("col")
    col_count = lax.axis_size("col")
    query_flat = lax.all_gather(units, "col", axis=0, tiled=True)
    block_lists = lax.all_gather(candidates, "col", axis=0, tiled=True)
    cand_flat, feat_flat = (
        lax.all_gather(units, "row", axis=0, tiled=True),
        lax.all_gather(features, "row", axis=0, tiled=True),
    )
    query_blocks = block_lists.shape[0]
    local = jnp.arange(query_blocks, dtype=jnp.int32)
    query_ids = (row_index * col_count + local // NB_DEV) * NB_DEV + local % NB_DEV
    holder = block_lists // NB_DEV
    keep = holder % col_count == col_index
    cand_local = holder // col_count * NB_DEV + block_lists % NB_DEV
    query_units = query_flat.reshape(-1, BLOCK, EMB)
    cand_units = cand_flat.reshape(-1, BLOCK, EMB)
    cand_feats = feat_flat.reshape(-1, BLOCK, FEAT)
    cand_sel, same_sel, counts = pair_lists(keep, cand_local, query_ids, block_lists)
    numerator, denominator = smooth_tile(
        query_units, cand_units, cand_feats, cand_sel, same_sel, counts
    )
    numerator, denominator = (
        lax.psum_scatter(numerator.reshape(-1, FEAT), "col", scatter_dimension=0, tiled=True),
        lax.psum_scatter(denominator.reshape(-1), "col", scatter_dimension=0, tiled=True),
    )
    return (numerator / denominator[:, None]).astype(jnp.bfloat16)


def solution(mesh):
    in_specs = (P(("row", "col"), None), P(("row", "col"), None), P(("row", "col"), None))
    out_specs = P(("row", "col"), None)
    return jax.shard_map(
        on_device, mesh=mesh, in_specs=in_specs, out_specs=out_specs, check_vma=False
    )
```

profile of v0, /device:TPU:0, one launch (start us, length us, event | category | flops | bytes accessed | tf_op | source)
XLA Modules:
  0.0 416.3 jit_solution(14212562513498291968)
XLA Ops:
  6.5 0.7 all-gather.9.cloned.1.call-update
  7.3 1.2 fusion.15
  8.5 2.0 fusion.16
  10.6 0.7 all-gather.7.cloned.1.call-update
  11.3 25.0 %all-gather = s32[16,2,38]{2,1,0:T(2,128)S(1)} all-gather(s32[1,2,38]{2,1,0:T(2,128)} %bitcast.38), channel_id=1, replica_groups=mesh['row'=8,'col'=16] {'col'}, dimensions={0}, use_global_device_ids=true | all-gather | bytes 5168 | tf_op jit(solution)/shard_map/all_gather | solution.py:78
  36.7 0.7 multiply_reduce_fusion
  37.5 0.7 and_reduce_fusion
  38.4 6.4 %scatter_custom_fusion = s32[1216]{0:T(1024)S(1)} fusion(s32[1216]{0:T(1024)S(1)} %reshape.115, s32[1216]{0:T(1024)S(1)} %reshape.117, s32[]{:T(128)} %constant.154.clone.1), kind=kCustom, calls=%fused_computation.58 | custom fusion | bytes 4868
  45.2 6.4 %scatter_custom_fusion.1 = s32[1216]{0:T(1024)S(1)} fusion(s32[1216]{0:T(1024)S(1)} %reshape.115, s32[1216]{0:T(1024)S(1)} %reshape.123, s32[]{:T(128)} %constant.154.clone.1), kind=kCustom, calls=%fused_computation.56 | custom fusion | bytes 4868
  51.8 0.7 reduce_max.9
  52.5 15.9 %all-gather.5.cloned.1.call-done = bf16[2048,1024]{1,0:T(8,128)(2,1)} async-done(((bf16[256,1024]{1,0:T(8,128)(2,1)}), bf16[2048,1024]{1,0:T(8,128)(2,1)}) %all-gather.5.cloned.1.call-update) | async-done | bytes 4194320 | tf_op jit(solution)/shard_map/all_gather | solution.py:80
  68.4 73.1 %all-gather.7.cloned.1.call-done = bf16[4096,1024]{1,0:T(8,128)(2,1)} async-done(((bf16[256,1024]{1,0:T(8,128)(2,1)}), bf16[4096,1024]{1,0:T(8,128)(2,1)}) %all-gather.7.cloned.1.call-update) | async-done | bytes 8388624 | tf_op jit(solution)/shard_map/all_gather | solution.py:77
  141.5 2.5 broadcast_in_dim.66
  144.0 47.2 %while.15 = (s32[]{:T(128)}, f32[32,128,256]{2,1,0:T(8,128)}, f32[32,128]{1,0:T(8,128)S(1)}, s32[]{:T(128)}, s32[32,38]{0,1:T(8,128)S(1)}, /*index=5*/s32[32,38]...) while((s32[]{:T(128)}, f32[32,128,256]{2,1,0:T(8,128)}, ...), condition=%wide.region_8.9_spmd.clone, body=%wide.region_6.8_spmd.clone.sunk | while | flops 1352156416 | bytes 50435528 | solution.py:69
  144.7 7.2 %gather_fusion.1 = bf16[32,128,1024]{2,1,0:T(8,128)(2,1)} fusion(bf16[16,128,1024]{2,1,0:T(8,128)(2,1)} %get-tuple-element.324, s32[1024]{0:T(1024)S(1)} %pad_clamp_fusion.2), kind=kCustom, calls=%fused_computation.clone.clone.1 | custom fusion | bytes 16777344 | tf_op jit(solution)/shard_map/while/body/jit(_take)/gather | solution.py:47
  151.9 9.3 %fusion.44 = (f32[32,128]{1,0:T(8,128)S(1)}, bf16[32,128,128]{1,2,0:T(8,128)(2,1)}) fusion(f32[32]{0:T(128)S(1)} %compare_convert_fusion.3, bf16[32,128,1024]{2,1,0:T(8,128)(2,1)} %get-tuple-element.325, bf16[32,128,1024]{2,1,0:T(8,128)(2,1)} %gather_fusion.1, pred[32]{0:T(512)(128)(4,1)S(1)} %get-tuple-element.289, ...), kind=kOutput, calls=%fused_computation.70.clone.1 | convolution fusion | flops 1081602048 | bytes 17858752 | tf_op jit(solution)/shard_map/while/body/qie,qje->qij/dot_general | solution.py:49
  161.3 0.7 gather_fusion
  162.0 5.3 %convolution_add_fusion.2 = f32[32,128,256]{2,1,0:T(8,128)} fusion(f32[32,128,256]{2,1,0:T(8,128)} %get-tuple-element.306, bf16[32,128,256]{2,1,0:T(8,128)(2,1)S(1)} %gather_fusion, pred[32]{0:T(512)(128)(4,1)S(1)} %get-tuple-element.289, bf16[32,128,128]{1,2,0:T(8,128)(2,1)} %get-tuple-element.290), kind=kOutput, calls=%fused_computation.9.clone.1 | convolution fusion | flops 270532608 | bytes 11534368 | tf_op jit(solution)/shard_map/while/body/qij,qjf->qif/dot_general | solution.py:55
  168.0 7.2 %gather_fusion.1 = bf16[32,128,1024]{2,1,0:T(8,128)(2,1)} fusion(bf16[16,128,1024]{2,1,0:T(8,128)(2,1)} %get-tuple-element.324, s32[1024]{0:T(1024)S(1)} %pad_clamp_fusion.2), kind=kCustom, calls=%fused_computation.clone.clone.1 | custom fusion | bytes 16777344 | tf_op jit(solution)/shard_map/while/body/jit(_take)/gather | solution.py:47
  175.2 9.3 %fusion.44 = (f32[32,128]{1,0:T(8,128)S(1)}, bf16[32,128,128]{1,2,0:T(8,128)(2,1)}) fusion(f32[32]{0:T(128)S(1)} %compare_convert_fusion.3, bf16[32,128,1024]{2,1,0:T(8,128)(2,1)} %get-tuple-element.325, bf16[32,128,1024]{2,1,0:T(8,128)(2,1)} %gather_fusion.1, pred[32]{0:T(512)(128)(4,1)S(1)} %get-tuple-element.289, ...), kind=kOutput, calls=%fused_computation.70.clone.1 | convolution fusion | flops 1081602048 | bytes 17858752 | tf_op jit(solution)/shard_map/while/body/qie,qje->qij/dot_general | solution.py:49
  185.2 5.3 %convolution_add_fusion.2 = f32[32,128,256]{2,1,0:T(8,128)} fusion(f32[32,128,256]{2,1,0:T(8,128)} %get-tuple-element.306, bf16[32,128,256]{2,1,0:T(8,128)(2,1)S(1)} %gather_fusion, pred[32]{0:T(512)(128)(4,1)S(1)} %get-tuple-element.289, bf16[32,128,128]{1,2,0:T(8,128)(2,1)} %get-tuple-element.290), kind=kOutput, calls=%fused_computation.9.clone.1 | convolution fusion | flops 270532608 | bytes 11534368 | tf_op jit(solution)/shard_map/while/body/qij,qjf->qif/dot_general | solution.py:55
  193.1 208.2 %all-reduce = f32[4096]{0:T(1024)S(1)} all-reduce(f32[4096]{0:T(1024)S(1)} %bitcast.34), channel_id=3, replica_groups=mesh['row'=8,'col'=16] {'col'}, use_global_device_ids=true, to_apply=%region_10.11.clone | all-reduce | flops 4096 | bytes 32768
  401.4 6.7 %reduce-scatter.2.cloned.1.call-done = f32[256,256]{1,0:T(8,128)} async-done(((f32[4096,256]{1,0:T(8,128)}), f32[256,256]{1,0:T(8,128)}) %reduce-scatter.2.cloned.1.call-update) | async-done | bytes 262160 | tf_op jit(solution)/shard_map/reduce_scatter | solution.py:97
  408.1 1.7 divide_convert_fusion
  (42 shorter events, 3.3 us)
Async XLA Ops:
  6.5 46.0 %all-gather.9.cloned.1.call-start = ((), (), s32[]{:S(2)}) async-start(), calls=%async_computation.3 | async-start | bytes 1179648 | tf_op jit(solution)/shard_map/all_gather | solution.py:81
  7.3 61.2 %all-gather.5.cloned.1.call-start = ((), (), s32[]{:S(2)}) async-start(), calls=%async_computation.1 | async-start | bytes 4718592 | tf_op jit(solution)/shard_map/all_gather | solution.py:80
  10.6 131.0 %all-gather.7.cloned.1.call-start = ((), (), s32[]{:S(2)}) async-start(), calls=%async_computation.2 | async-start | bytes 8912896 | tf_op jit(solution)/shard_map/all_gather | solution.py:77
  11.3 396.8 %reduce-scatter.2.cloned.1.call-start = ((), (), s32[]{:S(2)}) async-start(), calls=%async_computation.4 | async-start | bytes 4456448 | tf_op jit(solution)/shard_map/reduce_scatter | solution.py:97
  52.5 91.5 %copy-start = (bf16[2048,256]{1,0:T(8,128)(2,1)S(1)}, bf16[2048,256]{1,0:T(8,128)(2,1)}, u32[]{:S(2)}) copy-start(bf16[2048,256]{1,0:T(8,128)(2,1)} %all-gather.9.cloned.1.call-done) | copy-start | bytes 3145732
  191.2 0.7 copy-start.1
Sparse Core Ops, SparseCore 0:
  9.0 25.6 all-gather.8
  36.5 31.9 all-gather.4
  70.6 70.8 all-gather.6
  191.4 216.6 reduce-scatter.1
where the time goes:
time: 417 us; the launch traced here: 416 us
  blocking collectives  233 us (56%)
  waiting for transfers between devices  97.1 us (23%)
  local copies, waits for them, and re-layouts  33 us (8%)
  matrix products  29.2 us (7%)
  between operations  13.9 us (3%)
  other arithmetic  7.67 us (2%)
    unnamed x1, blocking collectives  208 us
    all_gather x1, waiting for transfers between devices, on_device(): query_flat = lax.all_gather(units, 'col', axis=0, tiled=True)  73.1 us
    all_gather x1, blocking collectives, on_device(): block_lists = lax.all_gather(candidates, 'col', axis=0, tiled=True)  25 us
    dot_general x2, matrix products, turn(): jnp.einsum('qie,qje->qij', query_units, cand_blk, preferred_element_type=...  18.6 us
    all_gather x1, waiting for transfers between devices, on_device(): lax.all_gather(units, 'row', axis=0, tiled=True)  15.9 us
    unnamed x11, local copies, waits for them, and re-layouts  14.4 us
    gather x2, local copies, waits for them, and re-layouts, turn(): cand_blk = jnp.take(cand_units, cand_idx, axis=0)  14.3 us
    dot_general x2, matrix products, turn(): jnp.einsum('qij,qjf->qif', weight.astype(jnp.bfloat16), feat_blk, preferr...  10.6 us
  transfers between devices with their start and end apart: 4, of which 3 were waited for; matrix products, arithmetic and copies ran while one was open for 5% of the time, Pallas kernels for 0%

commit v1 on v0

--- a/solution.py
+++ b/solution.py
@@ -77,7 +77,9 @@
     query_flat = lax.all_gather(units, "col", axis=0, tiled=True)
     block_lists = lax.all_gather(candidates, "col", axis=0, tiled=True)
     cand_flat, feat_flat = (
-        lax.all_gather(units, "row", axis=0, tiled=True),
+        jnp.concatenate(
+            lax.all_to_all(jnp.stack([units] * lax.axis_size("row")), "row", 0, 0), axis=0
+        ),
         lax.all_gather(features, "row", axis=0, tiled=True),
     )
     query_blocks = block_lists.shape[0]

time: 417 us -> 388 us (0.930)
  waiting for transfers between devices: 97.1 us -> 61 us
  starting transfers between devices: 0.12 us -> 4.76 us
    all_gather x1, waiting for transfers between devices: 73.1 us -> 39.7 us  [on_device(): query_flat = lax.all_gather(units, 'col', axis=0, tiled=True)]
    all_gather x1 -> x0, waiting for transfers between devices: 15.9 us -> none  [on_device(): lax.all_gather(units, 'row', axis=0, tiled=True)]
    all_to_all x0 -> x1, waiting for transfers between devices: none -> 13.9 us  [on_device(): lax.all_to_all(jnp.stack([units] * lax.axis_size('row')), 'row', 0, 0)]
    all_to_all x0 -> x1, starting transfers between devices: none -> 4.68 us  [on_device(): lax.all_to_all(jnp.stack([units] * lax.axis_size('row')), 'row', 0, 0)]
    unnamed x11 -> x17, local copies, waits for them, and re-layouts: 14.4 us -> 14.4 us
  transfers between devices with their start and end apart: 4 -> 4, of which waited for: 3 -> 3; matrix products, arithmetic and copies ran while one was open for 5% -> 6% of each run, Pallas kernels for 0% -> 0%
where the time goes in v1:
time: 388 us; the launch traced here: 387 us
  blocking collectives  233 us (60%)
  waiting for transfers between devices  61 us (16%)
  local copies, waits for them, and re-layouts  36.5 us (9%)
  matrix products  29.2 us (8%)
  between operations  13.9 us (4%)
  other arithmetic  6.35 us (2%)
  starting transfers between devices  4.76 us (1%)
    unnamed x1, blocking collectives  208 us
    all_gather x1, waiting for transfers between devices, on_device(): query_flat = lax.all_gather(units, 'col', axis=0, tiled=True)  39.7 us
    all_gather x1, blocking collectives, on_device(): block_lists = lax.all_gather(candidates, 'col', axis=0, tiled=True)  25 us
    dot_general x2, matrix products, turn(): jnp.einsum('qie,qje->qij', query_units, cand_blk, preferred_element_type=...  18.6 us
    unnamed x17, local copies, waits for them, and re-layouts  14.4 us
    gather x2, local copies, waits for them, and re-layouts, turn(): cand_blk = jnp.take(cand_units, cand_idx, axis=0)  14.3 us
    all_to_all x1, waiting for transfers between devices, on_device(): lax.all_to_all(jnp.stack([units] * lax.axis_size('row')), 'row', 0, 0)  13.9 us
    dot_general x2, matrix products, turn(): jnp.einsum('qij,qjf->qif', weight.astype(jnp.bfloat16), feat_blk, preferr...  10.6 us
  transfers between devices with their start and end apart: 4, of which 3 were waited for; matrix products, arithmetic and copies ran while one was open for 6% of the time, Pallas kernels for 0%

profile of v1, /device:TPU:0, one launch (start us, length us, event | category | flops | bytes accessed | tf_op | source)
XLA Modules:
  0.0 387.2 jit_solution(436440445017216651)
XLA Ops:
  6.5 0.7 all-gather.6.cloned.1.call-update
  7.3 1.2 fusion.15
  8.5 2.0 fusion.16
  10.5 3.6 stack.2
  14.1 4.7 %all-to-all-start = ((bf16[8,256,1024]{2,1,0:T(8,128)(2,1)}), bf16[8,256,1024]{2,1,0:T(8,128)(2,1)}, u32[]{:S(2)}, u32[]{:S(2)}) async-start(bf16[8,256,1024]{2,1,0:T(8,128)(2,1)} %stack.2), calls=%async_computation | async-start | bytes 8388608 | tf_op jit(solution)/shard_map/all_to_all | solution.py:81
  18.9 25.0 %all-gather = s32[16,2,38]{2,1,0:T(2,128)S(1)} all-gather(s32[1,2,38]{2,1,0:T(2,128)S(1)} %bitcast.37), channel_id=1, replica_groups=mesh['row'=8,'col'=16] {'col'}, dimensions={0}, use_global_device_ids=true | all-gather | bytes 5168 | tf_op jit(solution)/shard_map/all_gather | solution.py:78
  44.6 6.4 %scatter_custom_fusion = s32[1216]{0:T(1024)S(1)} fusion(s32[1216]{0:T(1024)S(1)} %reshape.113, s32[1216]{0:T(1024)S(1)} %reshape.115, s32[]{:T(128)} %constant.154.clone.1), kind=kCustom, calls=%fused_computation.58 | custom fusion | bytes 4868
  51.4 6.4 %scatter_custom_fusion.1 = s32[1216]{0:T(1024)S(1)} fusion(s32[1216]{0:T(1024)S(1)} %reshape.113, s32[1216]{0:T(1024)S(1)} %reshape.121, s32[]{:T(128)} %constant.154.clone.1), kind=kCustom, calls=%fused_computation.56 | custom fusion | bytes 4868
  58.0 0.7 reduce_max.9
  58.8 13.9 %all-to-all-done = bf16[8,256,1024]{2,1,0:T(8,128)(2,1)} async-done(((bf16[8,256,1024]{2,1,0:T(8,128)(2,1)}), bf16[8,256,1024]{2,1,0:T(8,128)(2,1)}, u32[]{:S(2)}, u32[]{:S(2)}) %all-to-all-start) | async-done | bytes 4194336 | tf_op jit(solution)/shard_map/all_to_all | solution.py:81
  72.6 39.7 %all-gather.4.cloned.1.call-done = bf16[4096,1024]{1,0:T(8,128)(2,1)} async-done(((bf16[256,1024]{1,0:T(8,128)(2,1)}), bf16[4096,1024]{1,0:T(8,128)(2,1)}) %all-gather.4.cloned.1.call-update) | async-done | bytes 8388624 | tf_op jit(solution)/shard_map/all_gather | solution.py:77
  112.3 2.5 broadcast_in_dim.66
  114.8 47.2 %while.15 = (s32[]{:T(128)}, f32[32,128,256]{2,1,0:T(8,128)}, f32[32,128]{1,0:T(8,128)S(1)}, s32[]{:T(128)}, s32[32,38]{0,1:T(8,128)S(1)}, /*index=5*/s32[32,38]...) while((s32[]{:T(128)}, f32[32,128,256]{2,1,0:T(8,128)}, ...), condition=%wide.region_8.9_spmd.clone, body=%wide.region_6.8_spmd.clone.sunk | while | flops 1352156416 | bytes 50435528 | solution.py:69
  115.5 7.2 %gather_fusion.1 = bf16[32,128,1024]{2,1,0:T(8,128)(2,1)} fusion(bf16[16,128,1024]{2,1,0:T(8,128)(2,1)} %get-tuple-element.324, s32[1024]{0:T(1024)S(1)} %pad_clamp_fusion.2), kind=kCustom, calls=%fused_computation.clone.clone.1 | custom fusion | bytes 16777344 | tf_op jit(solution)/shard_map/while/body/jit(_take)/gather | solution.py:47
  122.7 9.3 %fusion.44 = (f32[32,128]{1,0:T(8,128)S(1)}, bf16[32,128,128]{1,2,0:T(8,128)(2,1)}) fusion(f32[32]{0:T(128)S(1)} %compare_convert_fusion.3, bf16[32,128,1024]{2,1,0:T(8,128)(2,1)} %get-tuple-element.325, bf16[32,128,1024]{2,1,0:T(8,128)(2,1)} %gather_fusion.1, pred[32]{0:T(512)(128)(4,1)S(1)} %get-tuple-element.289, ...), kind=kOutput, calls=%fused_computation.70.clone.1 | convolution fusion | flops 1081602048 | bytes 17858752 | tf_op jit(solution)/shard_map/while/body/qie,qje->qij/dot_general | solution.py:49
  132.0 0.7 gather_fusion
  132.7 5.3 %convolution_add_fusion.2 = f32[32,128,256]{2,1,0:T(8,128)} fusion(f32[32,128,256]{2,1,0:T(8,128)} %get-tuple-element.306, bf16[32,128,256]{2,1,0:T(8,128)(2,1)S(1)} %gather_fusion, pred[32]{0:T(512)(128)(4,1)S(1)} %get-tuple-element.289, bf16[32,128,128]{1,2,0:T(8,128)(2,1)} %get-tuple-element.290), kind=kOutput, calls=%fused_computation.9.clone.1 | convolution fusion | flops 270532608 | bytes 11534368 | tf_op jit(solution)/shard_map/while/body/qij,qjf->qif/dot_general | solution.py:55
  138.8 7.2 %gather_fusion.1 = bf16[32,128,1024]{2,1,0:T(8,128)(2,1)} fusion(bf16[16,128,1024]{2,1,0:T(8,128)(2,1)} %get-tuple-element.324, s32[1024]{0:T(1024)S(1)} %pad_clamp_fusion.2), kind=kCustom, calls=%fused_computation.clone.clone.1 | custom fusion | bytes 16777344 | tf_op jit(solution)/shard_map/while/body/jit(_take)/gather | solution.py:47
  146.0 9.3 %fusion.44 = (f32[32,128]{1,0:T(8,128)S(1)}, bf16[32,128,128]{1,2,0:T(8,128)(2,1)}) fusion(f32[32]{0:T(128)S(1)} %compare_convert_fusion.3, bf16[32,128,1024]{2,1,0:T(8,128)(2,1)} %get-tuple-element.325, bf16[32,128,1024]{2,1,0:T(8,128)(2,1)} %gather_fusion.1, pred[32]{0:T(512)(128)(4,1)S(1)} %get-tuple-element.289, ...), kind=kOutput, calls=%fused_computation.70.clone.1 | convolution fusion | flops 1081602048 | bytes 17858752 | tf_op jit(solution)/shard_map/while/body/qie,qje->qij/dot_general | solution.py:49
  155.3 0.7 gather_fusion
  156.0 5.3 %convolution_add_fusion.2 = f32[32,128,256]{2,1,0:T(8,128)} fusion(f32[32,128,256]{2,1,0:T(8,128)} %get-tuple-element.306, bf16[32,128,256]{2,1,0:T(8,128)(2,1)S(1)} %gather_fusion, pred[32]{0:T(512)(128)(4,1)S(1)} %get-tuple-element.289, bf16[32,128,128]{1,2,0:T(8,128)(2,1)} %get-tuple-element.290), kind=kOutput, calls=%fused_computation.9.clone.1 | convolution fusion | flops 270532608 | bytes 11534368 | tf_op jit(solution)/shard_map/while/body/qij,qjf->qif/dot_general | solution.py:55
  163.9 208.3 %all-reduce = f32[4096]{0:T(1024)S(1)} all-reduce(f32[4096]{0:T(1024)S(1)} %bitcast.33), channel_id=3, replica_groups=mesh['row'=8,'col'=16] {'col'}, use_global_device_ids=true, to_apply=%region_10.11.clone | all-reduce | flops 4096 | bytes 32768
  372.3 6.7 %reduce-scatter.2.cloned.1.call-done = f32[256,256]{1,0:T(8,128)} async-done(((f32[4096,256]{1,0:T(8,128)}), f32[256,256]{1,0:T(8,128)}) %reduce-scatter.2.cloned.1.call-update) | async-done | bytes 262160 | tf_op jit(solution)/shard_map/reduce_scatter | solution.py:99
  378.9 1.7 divide_convert_fusion
  (48 shorter events, 2.8 us)
Async XLA Ops:
  6.5 52.2 %all-gather.6.cloned.1.call-start = ((), (), s32[]{:S(2)}) async-start(), calls=%async_computation.3 | async-start | bytes 1179648 | tf_op jit(solution)/shard_map/all_gather | solution.py:83
  7.3 105.1 %all-gather.4.cloned.1.call-start = ((), (), s32[]{:S(2)}) async-start(), calls=%async_computation.2 | async-start | bytes 8912896 | tf_op jit(solution)/shard_map/all_gather | solution.py:77
  14.1 4.8 %copy-start.1 = (s32[2,38]{1,0:T(2,128)S(1)}, s32[2,38]{1,0:T(2,128)}, u32[]{:S(2)}) copy-start(s32[2,38]{1,0:T(2,128)} %param.7) | copy-start | bytes 916
  14.1 30.1 %copy-start.3 = (s32[2]{0:T(128)S(1)}, s32[2]{0:T(128)}, u32[]{:S(2)}) copy-start(s32[2]{0:T(128)} %constant.171) | copy-start | bytes 28
  14.1 30.2 %copy-start.2 = (s32[2]{0:T(128)S(1)}, s32[2]{0:T(128)}, u32[]{:S(2)}) copy-start(s32[2]{0:T(128)} %constant.174) | copy-start | bytes 28
  14.1 58.5 %all-to-all-start = ((bf16[8,256,1024]{2,1,0:T(8,128)(2,1)}), bf16[8,256,1024]{2,1,0:T(8,128)(2,1)}, u32[]{:S(2)}, u32[]{:S(2)}) async-start(bf16[8,256,1024]{2,1,0:T(8,128)(2,1)} %stack.2), calls=%async_computation | async-start | bytes 8388608 | tf_op jit(solution)/shard_map/all_to_all | solution.py:81
  18.8 360.1 %reduce-scatter.2.cloned.1.call-start = ((), (), s32[]{:S(2)}) async-start(), calls=%async_computation.4 | async-start | bytes 4456448 | tf_op jit(solution)/shard_map/reduce_scatter | solution.py:99
  58.7 56.0 %copy-start = (bf16[2048,256]{1,0:T(8,128)(2,1)S(1)}, bf16[2048,256]{1,0:T(8,128)(2,1)}, u32[]{:S(2)}) copy-start(bf16[2048,256]{1,0:T(8,128)(2,1)} %all-gather.6.cloned.1.call-done) | copy-start | bytes 3145732
  162.0 0.7 copy-start.4
Sparse Core Ops, SparseCore 0:
  9.0 29.8 all-gather.5
  41.1 71.1 all-gather.3
  162.1 216.7 reduce-scatter.1
